TPU v7x, 32 devices: a whole 2x2x4 slice. The times are simulated.
32 devices in a mesh: case: 2 (over x), ax: 16 (over z, y, core).
Axes of the slice: x: 2, y: 2, z: 4, core: 2. Of those that a mesh axis runs over, the one named last changes fastest.
Arguments:
- populations: float32 [19, 32, 128, 128], P(None, 'ax', 'case'), parts along dimension 2, may hold values from 0 to 1, as said below
- solid_mask: int32 [32, 128, 128], P('ax', 'case'), parts along dimension 1, may hold values from 0 to 1, as said below
- link_flags: int32 [2, 32, 128, 128], P(None, 'ax', 'case'), parts along dimension 2, may hold values from 0 to 511, as said below
- inlet_cells: int32 [1024], P('case'), parts along dimension 0, may hold values from 0 to 8191, as said below
- pod_basis: float32 [512, 3, 512], P(None, None, 'ax'), may hold values from -0.15625 to 0.15625
- mri_frames: float32 [24, 6, 512], P(None, 'case', 'ax'), parts along dimension 1
- frame_index: int32 [1], replicated, may hold values from 0 to 23
Outputs:
- advanced_populations: float32 [19, 32, 128, 128], P(None, 'ax', 'case'), parts along dimension 2
- inflow: float32 [2, 6, 512], P(None, 'case', 'ax'), parts along dimension 1
There are 2 independent parts, one for each index of `case`. A program takes and returns all parts, laid end to end along the dimension named above; an argument that names none is the same for every part. Nothing has to cross between parts.
Inputs may be any that keep to these rules, and one draw needn't show every extreme that they name: `solid_mask`: 1 marks a wall cell, 0 a fluid cell; the two outermost rows and columns of every cross-section are wall cells. `link_flags`: at a fluid cell, bit (i - 1) mod 9 of word (i - 1) div 9 is set exactly when the cell at minus c_i is a wall cell, the grid being continued past its first and last plane by repeating those planes; zero at wall cells. `inlet_cells`: distinct cells of the first plane, all of them fluid cells. `populations`: every entry is positive.
All inputs are finite; a program needn't handle non-finite values.
Results may differ from a plain program's by a relative error of at most 0.00011.
Values sent between devices are 32-bit elements; how exact they have to be, the bound alone decides.
A program may use at most 64 MiB of HBM per device.

v0:
```python
import math
import jax
import jax.numpy as jnp
from jax import lax
from jax.sharding import PartitionSpec as P

STEPS = 2
lattice_c = (
    (0, 0, 0),
    (1, 0, 0),
    (-1, 0, 0),
    (0, 1, 0),
    (0, -1, 0),
    (0, 0, 1),
    (0, 0, -1),
    (1, 1, 0),
    (-1, -1, 0),
    (1, -1, 0),
    (-1, 1, 0),
    (1, 0, 1),
    (-1, 0, -1),
    (1, 0, -1),
    (-1, 0, 1),
    (0, 1, 1),
    (0, -1, -1),
    (0, 1, -1),
    (0, -1, 1),
)
lattice_w = (1.0 / 3.0,) + (1.0 / 18.0,) * 6 + (1.0 / 36.0,) * 12
opposite_of = (0, 2, 1, 4, 3, 6, 5, 8, 7, 10, 9, 12, 11, 14, 13, 16, 15, 18, 17)
pair_list = ((0, 0), (1, 1), (2, 2), (0, 1), (0, 2), (1, 2))
relax_base = 0.52
smagorinsky_sq = 0.04
inflow_scale = 0.05


def extended(array, sides, width):
    for axis, dim in sides:
        count, length = (lax.axis_size(axis), array.shape[dim])
        up = [(i, (i + 1) % count) for i in range(count - 1)]
        down = [(j, i) for i, j in up]
        last = lax.slice_in_dim(array, length - width, length, axis=dim)
        leading = lax.slice_in_dim(array, 0, width, axis=dim)
        before = lax.ppermute(last, axis, up)
        after = lax.ppermute(leading, axis, down)
        array = jnp.concatenate([before, array, after], axis=dim)
    return array


def moment_rows():
    listed = [[1.0] * 19]
    for axis_a in range(3):
        listed.append([float(vector[axis_a]) for vector in lattice_c])
    for pair_a, pair_b in pair_list:
        listed.append([float(vector[pair_a] * vector[pair_b]) for vector in lattice_c])
    return jnp.asarray(listed, dtype=jnp.float32)


def equilibrium(density, velocity):
    lattice = jnp.asarray(
        [[float(entry) for entry in vector] for vector in lattice_c], dtype=jnp.float32
    )
    weights = jnp.asarray(list(lattice_w), dtype=jnp.float32).reshape((19,) + (1,) * density.ndim)
    projected = jnp.einsum("iq,q...->i...", lattice, velocity, precision=lax.Precision.HIGHEST)
    speed_sq = jnp.sum(velocity * velocity, axis=0)
    return (
        weights
        * density[None]
        * (1.0 + 3.0 * projected + 4.5 * projected * projected - 1.5 * speed_sq[None])
    )


def collide(populations, solid_mask):
    moments = jnp.einsum(
        "mi,i...->m...", moment_rows(), populations, precision=lax.Precision.HIGHEST
    )
    density = moments[0]
    velocity = moments[1:4] / density[None]
    nonequil = populations - equilibrium(density, velocity)
    stress = jnp.einsum(
        "mi,i...->m...", moment_rows()[4:], nonequil, precision=lax.Precision.HIGHEST
    )
    magnitude = stress[0] * stress[0] + stress[1] * stress[1] + stress[2] * stress[2]
    magnitude = magnitude + 2.0 * (
        stress[3] * stress[3] + stress[4] * stress[4] + stress[5] * stress[5]
    )
    relax_time = 0.5 * (
        relax_base
        + jnp.sqrt(
            relax_base * relax_base
            + 18.0 * math.sqrt(2.0) * smagorinsky_sq * jnp.sqrt(magnitude) / density
        )
    )
    relaxed = populations - nonequil / relax_time[None]
    return jnp.where(solid_mask[None] == 1, populations, relaxed)


def stream(relaxed, ghost_low, ghost_high, link_flags, solid_mask):
    padded = jnp.concatenate([ghost_low[:, None], relaxed, ghost_high[:, None]], axis=1)
    planes_here = relaxed.shape[1]
    read = []
    for direction in range(19):
        step_x, step_y, step_z = lattice_c[direction]
        source = padded[direction, 1 - step_z : 1 - step_z + planes_here]
        source = jnp.roll(source, (step_y, step_x), axis=(1, 2))
        if direction > 0:
            word = link_flags[(direction - 1) // 9]
            linked = jnp.bitwise_and(jnp.right_shift(word, (direction - 1) % 9), 1)
            source = jnp.where(linked == 1, relaxed[opposite_of[direction]], source)
        read.append(jnp.where(solid_mask == 1, relaxed[direction], source))
    return jnp.stack(read)


def inlet_plane(speeds, inlet_cells, height, plane_width):
    inlet_speed = jnp.zeros((3, height * plane_width), jnp.float32).at[:, inlet_cells].set(speeds)
    inlet_speed = inlet_speed.reshape(3, height, plane_width)
    return equilibrium(jnp.ones((height, plane_width), jnp.float32), inlet_speed)


def neighbour_planes(relaxed):
    padded = extended(relaxed, (("ax", 1),), 1)
    ghost_low = padded[:, 0]
    ghost_high = padded[:, -1]
    return (ghost_low, ghost_high)


def body(populations, solid_mask, link_flags, inlet_cells, pod_basis, mri_frames, frame_index):
    frames_total = mri_frames.shape[0]
    frame_slot = lax.broadcasted_iota(jnp.int32, (STEPS, frames_total), 1)
    segment_slot = lax.broadcasted_iota(jnp.int32, (STEPS, frames_total), 0)
    selector = (frame_slot == (frame_index[0] + segment_slot) % frames_total).astype(jnp.float32)
    chosen = jnp.einsum("sf,fjc->sjc", selector, mri_frames, precision=lax.Precision.HIGHEST)
    partial_terms = jnp.einsum("kjc,sjc->sk", pod_basis, chosen, precision=lax.Precision.HIGHEST)
    coefficients = lax.psum(partial_terms, "ax")
    local_inflow = jnp.einsum(
        "kjc,sk->sjc", pod_basis, coefficients, precision=lax.Precision.HIGHEST
    )
    whole_inflow = lax.all_gather(local_inflow, "ax", axis=2, tiled=True)
    position = lax.axis_index("ax")
    axis_count = lax.axis_size("ax")
    height = populations.shape[2]
    plane_width = populations.shape[3]
    for segment_index in range(STEPS):
        relaxed = collide(populations, solid_mask)
        inlet_ghost = inlet_plane(
            inflow_scale * whole_inflow[segment_index], inlet_cells, height, plane_width
        )
        ghost_low, ghost_high = neighbour_planes(relaxed)
        ghost_low = jnp.where(position == 0, inlet_ghost, ghost_low)
        ghost_high = jnp.where(position == axis_count - 1, relaxed[:, -1], ghost_high)
        populations = stream(relaxed, ghost_low, ghost_high, link_flags, solid_mask)
    return (populations, local_inflow)


def solution(mesh):
    in_specs = (
        P(None, "ax", "case", None),
        P("ax", "case", None),
        P(None, "ax", "case", None),
        P("case"),
        P(None, None, "ax"),
        P(None, "case", "ax"),
        P(),
    )
    out_specs = (P(None, "ax", "case", None), P(None, "case", "ax"))
    return jax.shard_map(body, mesh=mesh, in_specs=in_specs, out_specs=out_specs, check_vma=False)
```

profile of v0, /device:TPU:1, one launch (start us, length us, event | category | flops | bytes accessed | tf_op | source)
XLA Modules:
  0.0 146.1 jit_solution(2449302820524212767)
XLA Ops:
  0.6 0.9 broadcast_compare_fusion
  1.6 3.0 %fusion.4 = f32[10,2,64,128]{3,0,2,1:T(8,128)S(1)} fusion(f32[10,19,1,1]{1,0,3,2:T(8,128)} %constant.81, f32[19,2,64,128]{3,2,1,0:T(8,128)} %param.19), kind=kOutput, calls=%fused_computation.12 | convolution fusion | flops 37355520 | bytes 1901304 | tf_op jit(solution)/shard_map/mi,i...->m.../dot_general | solution.py:74
  4.9 1.5 %fusion.149 = f32[19,2,64,128]{3,0,2,1:T(8,128)S(1)} fusion(f32[19,3,1,1]{0,1,3,2:T(4,128)S(1)} %copy-done.22, f32[10,2,64,128]{3,0,2,1:T(8,128)S(1)} %fusion.4, f32[2,64,128]{2,1,0:T(8,128)S(1)} %bitcast.600), kind=kOutput, calls=%fused_computation.338 | convolution fusion | flops 11255808 | bytes 1574912 | tf_op jit(solution)/shard_map/iq,q...->i.../dot_general | solution.py:64
  6.4 0.4 copy_multiply_fusion.2
  6.8 0.8 copy-done.3
  7.7 2.8 %copy_subtract_fusion = f32[19,2,64,128]{3,0,2,1:T(8,128)S(1)} fusion(f32[19,2,64,128]{3,2,1,0:T(8,128)S(1)} %copy-done.3, f32[19,2,64,128]{3,2,1,0:T(8,128)S(1)} %get-tuple-element.100, f32[19,2,64,128]{3,2,1,0:T(8,128)S(1)} %get-tuple-element.61, f32[19,2,64,128]{3,0,2,1:T(8,128)S(1)} %fusion.149, f32[19,2,64,128]{3,2,1,0:T(8,128)S(1)} %get-tuple-element.60, ...), kind=kLoop, calls=%fused_computation.11 | loop fusion | flops 1556480 | bytes 7536640 | tf_op jit(solution)/shard_map/sub | solution.py:79
  10.5 0.9 fusion.171
  11.5 0.3 fusion.170
  11.9 1.0 subtract_select_fusion
  13.1 0.9 copy-done.5
  14.1 2.1 %collective-permute-start.1 = (f32[19,1,64,128]{3,2,1,0:T(8,128)S(1)}, f32[19,1,64,128]{3,2,1,0:T(8,128)}, u32[]{:S(2)}, u32[]{:S(2)}) collective-permute-start(f32[19,1,64,128]{3,2,1,0:T(8,128)S(1)} %slice.827), channel_id=1, source_target_pairs={{1,0},{2,1},{3,2},{4,3},{5,4},{6,5},{7,6},{8,7},{9,8},{10,9},{11,1... | collective-permute-start | bytes 1867784 | tf_op jit(solution)/shard_map/ppermute | solution.py:45
  16.1 0.6 slice_bitcast_fusion.36
  18.0 31.4 %psum.7 = f32[2,512]{1,0:T(2,128)S(1)} all-reduce(f32[2,512]{1,0:T(2,128)S(1)} %convolution_bitcast_fusion), channel_id=1, replica_groups=mesh['case'=2,'ax'=16] {'ax'}, use_global_device_ids=true, to_apply=%region_1.2 | all-reduce | flops 1024 | bytes 8192 | tf_op jit(solution)/shard_map/psum | solution.py:134
  49.3 1.0 fusion.139
  50.4 0.5 compare_select_fusion
  50.9 0.8 copy.150
  51.7 23.9 %all_gather.3 = f32[2,3,512]{1,0,2:T(2,128)S(1)} all-gather(f32[2,3,32]{1,0,2:T(2,128)S(1)} %copy.150), channel_id=1, replica_groups=mesh['case'=2,'ax'=16] {'ax'}, dimensions={2}, use_global_device_ids=true | all-gather | bytes 13056 | tf_op jit(solution)/shard_map/all_gather | solution.py:138
  75.6 1.4 slice_multiply_fusion
  77.1 0.6 constant_dynamic-update-slice_fusion.17
  77.7 0.6 copy-done.9
  78.3 0.7 slice.815
  79.0 4.3 %scatter_custom_fusion = f32[3,8192]{0,1:T(8,128)} fusion(s32[512]{0:T(512)} %compare_select_fusion, f32[512,3]{1,0:T(8,128)} %bitcast.636, f32[]{:T(128)} %constant.31.clone.1), kind=kCustom, calls=%fused_computation.7 | custom fusion | bytes 98816 | tf_op jit(solution)/shard_map/scatter | solution.py:115
  83.4 3.4 %multiply_reduce_fusion.1 = f32[8192]{0:T(1024)S(1)} fusion(f32[3,8192]{0,1:T(8,128)} %scatter_custom_fusion), kind=kLoop, calls=%fused_computation.3 | loop fusion | flops 40960 | bytes 131072 | tf_op jit(solution)/shard_map/reduce_sum | solution.py:65
  86.7 0.6 constant_dynamic-update-slice_fusion.16
  87.4 0.6 constant_dynamic-update-slice_fusion.15
  88.0 0.6 multiply_bitcast_fusion.3
  88.6 4.3 %scatter_custom_fusion.1 = f32[3,8192]{0,1:T(8,128)} fusion(s32[512]{0:T(512)} %compare_select_fusion, f32[512,3]{1,0:T(8,128)} %bitcast.635, f32[]{:T(128)} %constant.31.clone.1), kind=kCustom, calls=%fused_computation.5 | custom fusion | bytes 98816 | tf_op jit(solution)/shard_map/scatter | solution.py:115
  92.9 3.5 %multiply_reduce_fusion = f32[8192]{0:T(1024)S(1)} fusion(f32[3,8192]{0,1:T(8,128)} %scatter_custom_fusion.1), kind=kLoop, calls=%fused_computation.2 | loop fusion | flops 40960 | bytes 131072 | tf_op jit(solution)/shard_map/reduce_sum | solution.py:65
  96.4 4.6 %fusion.172 = f32[19,64,128]{2,0,1:T(8,128)} fusion(f32[19,3,1]{0,1,2:T(4,128)S(1)} %copy-done.24, f32[3,64,128]{0,2,1:T(8,128)S(1)} %bitcast.598), kind=kOutput, calls=%fused_computation.343 | convolution fusion | flops 5603328 | bytes 721124 | tf_op jit(solution)/shard_map/iq,q...->i.../dot_general | solution.py:64
  101.0 2.0 %bitcast_select_fusion = (f32[19,1,64,128]{3,2,1,0:T(8,128)S(1)}, f32[19,1,64,128]{3,2,1,0:T(8,128)}) fusion(f32[19,1,64,128]{3,2,1,0:T(8,128)} %collective-permute-done.1, pred[]{:T(512)S(6)} %eq.197, f32[19,2,64,128]{3,2,1,0:T(8,128)S(1)} %copy.143), kind=kLoop, calls=%fused_computation.45 | loop fusion | flops 155648 | bytes 2490369 | tf_op jit(solution)/shard_map/jit(_where)/select_n | solution.py:150
  103.1 3.9 %collective-permute-start = (f32[19,1,64,128]{3,2,1,0:T(8,128)}, f32[19,1,64,128]{3,2,1,0:T(8,128)}, u32[]{:S(2)}, u32[]{:S(2)}) collective-permute-start(f32[19,1,64,128]{3,2,1,0:T(8,128)} %get-tuple-element.80), channel_id=1, source_target_pairs={{0,1},{1,2},{2,3},{3,4},{4,5},{5,6},{6,7},{7,8},{8,9},{9,10},{10,1... | collective-permute-start | bytes 1867784 | tf_op jit(solution)/shard_map/ppermute | solution.py:44
  107.0 1.7 %slice.867 = f32[1,2,64,128]{3,0,2,1:T(1,128)} slice(f32[19,2,64,128]{3,0,2,1:T(8,128)} %copy-done.5), slice={[18:19], [0:2], [0:64], [0:128]} | slice | bytes 131072 | tf_op jit(solution)/shard_map/slice | solution.py:109
  108.8 0.6 slice.822
  109.3 0.6 slice.821
  110.0 0.9 constant_dynamic-update-slice_fusion.14
  110.9 5.6 %fusion.173 = f32[19,64,128]{2,0,1:T(8,128)S(1)} fusion(f32[19,3,1]{0,1,2:T(4,128)} %constant.84, f32[3,64,128]{0,2,1:T(8,128)} %bitcast.597), kind=kOutput, calls=%fused_computation.344 | convolution fusion | flops 5603328 | bytes 721124 | tf_op jit(solution)/shard_map/iq,q...->i.../dot_general | solution.py:64
  116.5 1.3 fusion.19
  119.6 0.4 copy-done.7
  120.2 1.7 %fusion.8 = f32[10,2,64,128]{3,0,2,1:T(8,128)S(1)} fusion(f32[10,19,1,1]{1,0,3,2:T(8,128)S(1)} %copy-done.19, f32[19,2,64,128]{3,2,1,0:T(8,128)S(1)} %get-tuple-element.2), kind=kOutput, calls=%fused_computation.16 | convolution fusion | flops 37355520 | bytes 1901304 | tf_op jit(solution)/shard_map/mi,i...->m.../dot_general | solution.py:74
  122.2 1.5 %fusion.150 = f32[19,2,64,128]{3,0,2,1:T(8,128)S(1)} fusion(f32[19,3,1,1]{0,1,3,2:T(4,128)S(1)} %copy-done.23, f32[10,2,64,128]{3,0,2,1:T(8,128)S(1)} %fusion.8, f32[2,64,128]{2,1,0:T(8,128)S(1)} %bitcast.604), kind=kOutput, calls=%fused_computation.339 | convolution fusion | flops 11255808 | bytes 1574912 | tf_op jit(solution)/shard_map/iq,q...->i.../dot_general | solution.py:64
  123.7 0.4 fusion.14
  124.4 1.6 %fusion.6 = f32[6,2,64,128]{3,0,2,1:T(8,128)S(1)} fusion(f32[6,19,1,1]{1,0,3,2:T(8,128)S(1)} %copy-done.21, f32[19,2,64,128]{3,2,1,0:T(8,128)S(1)} %fusion.14), kind=kOutput, calls=%fused_computation.14 | convolution fusion | flops 22413312 | bytes 1638856 | tf_op jit(solution)/shard_map/mi,i...->m.../dot_general | solution.py:80
  126.0 0.3 fusion.169
  126.4 0.3 subtract_select_fusion.1
  126.8 2.3 %collective-permute-start.2 = (f32[19,1,64,128]{3,2,0,1:T(8,128)S(1)}, f32[19,1,64,128]{3,2,0,1:T(8,128)S(1)}, u32[]{:S(2)}, u32[]{:S(2)}) collective-permute-start(f32[19,1,64,128]{3,2,0,1:T(8,128)S(1)} %get-tuple-element.67), channel_id=1, source_target_pairs={{0,1},{1,2},{2,3},{3,4},{4,5},{5,6},{6,7},{7,8},{8,9},{9,10},{10,1... | collective-permute-start | bytes 1867784 | tf_op jit(solution)/shard_map/ppermute | solution.py:44
  129.6 2.1 %collective-permute-start.3 = (f32[19,1,64,128]{3,2,0,1:T(8,128)S(1)}, f32[19,1,64,128]{3,2,0,1:T(8,128)S(1)}, u32[]{:S(2)}, u32[]{:S(2)}) collective-permute-start(f32[19,1,64,128]{3,2,0,1:T(8,128)S(1)} %get-tuple-element.66), channel_id=1, source_target_pairs={{1,0},{2,1},{3,2},{4,3},{5,4},{6,5},{7,6},{8,7},{9,8},{10,9},{11,1... | collective-permute-start | bytes 1867784 | tf_op jit(solution)/shard_map/ppermute | solution.py:45
  131.7 11.2 %collective-permute-done.2 = f32[19,1,64,128]{3,2,0,1:T(8,128)S(1)} collective-permute-done((f32[19,1,64,128]{3,2,0,1:T(8,128)S(1)}, f32[19,1,64,128]{3,2,0,1:T(8,128)S(1)}, u32[]{:S(2)}, u32[]{:S(2)}) %collective-permute-start.2) | collective-permute-done | bytes 622624 | tf_op jit(solution)/shard_map/ppermute | solution.py:44
  145.1 1.0 copy-done.27
  (156 shorter events, 6.2 us)
Async XLA Ops:
  0.6 17.1 %copy-start = (f32[512,3,32]{0,2,1:T(8,128)S(1)}, f32[512,3,32]{0,2,1:T(8,128)}, u32[]{:S(2)}) copy-start(f32[512,3,32]{0,2,1:T(8,128)} %param.23) | copy-start | bytes 589828
  1.5 3.3 %copy-start.22 = (f32[19,3,1,1]{0,1,3,2:T(4,128)S(1)}, f32[19,3,1,1]{0,1,3,2:T(4,128)}, u32[]{:S(2)}) copy-start(f32[19,3,1,1]{0,1,3,2:T(4,128)} %constant.82) | copy-start | bytes 688
  4.8 1.5 %copy-start.25 = (f32[19]{0:T(128)S(1)}, f32[19]{0:T(128)}, u32[]{:S(2)}) copy-start(f32[19]{0:T(128)} %constant.24.clone) | copy-start | bytes 232
  6.4 1.3 copy-start.3
  7.7 2.8 %copy-start.20 = (f32[6,19,1,1]{1,0,3,2:T(8,128)S(1)}, f32[6,19,1,1]{1,0,3,2:T(8,128)}, u32[]{:S(2)}) copy-start(f32[6,19,1,1]{1,0,3,2:T(8,128)} %constant.83) | copy-start | bytes 1372
  12.8 1.2 copy-start.5
  14.0 3.5 %copy-start.29 = (f32[24,3,32]{2,0,1:T(8,128)S(1)}, f32[24,3,32]{2,0,1:T(8,128)}, u32[]{:S(2)}) copy-start(f32[24,3,32]{2,0,1:T(8,128)} %param.24) | copy-start | bytes 27652
  14.0 36.4 %copy-start.28 = (s32[512]{0:T(512)S(1)}, s32[512]{0:T(512)}, u32[]{:S(2)}) copy-start(s32[512]{0:T(512)} %param.22) | copy-start | bytes 6148
  14.1 87.0 %collective-permute-start.1 = (f32[19,1,64,128]{3,2,1,0:T(8,128)S(1)}, f32[19,1,64,128]{3,2,1,0:T(8,128)}, u32[]{:S(2)}, u32[]{:S(2)}) collective-permute-start(f32[19,1,64,128]{3,2,1,0:T(8,128)S(1)} %slice.827), channel_id=1, source_target_pairs={{1,0},{2,1},{3,2},{4,3},{5,4},{6,5},{7,6},{8,7},{9,8},{10,9},{11,1... | collective-permute-start | bytes 1867784 | tf_op jit(solution)/shard_map/ppermute | solution.py:45
  16.8 60.3 %copy-start.1 = (s32[2,64,128]{2,1,0:T(8,128)S(1)}, s32[2,64,128]{2,1,0:T(8,128)}, u32[]{:S(2)}) copy-start(s32[2,64,128]{2,1,0:T(8,128)} %param.20) | copy-start | bytes 196612
  16.8 60.3 %copy-start.4 = (s32[2,2,64,128]{3,2,1,0:T(8,128)S(1)}, s32[2,2,64,128]{3,2,1,0:T(8,128)}, u32[]{:S(2)}) copy-start(s32[2,2,64,128]{3,2,1,0:T(8,128)} %param.21) | copy-start | bytes 393220
  51.7 25.3 %copy-start.8 = (f32[2,64,128]{2,1,0:T(8,128)S(1)}, f32[2,64,128]{2,1,0:T(8,128)}, u32[]{:S(2)}) copy-start(f32[2,64,128]{2,1,0:T(8,128)} %get-tuple-element.84) | copy-start | bytes 196612
  77.7 0.6 copy-start.9
  77.7 1.3 copy-start.12
  83.3 3.4 %copy-start.10 = (f32[2,64,128]{2,1,0:T(8,128)S(1)}, f32[2,64,128]{2,1,0:T(8,128)}, u32[]{:S(2)}) copy-start(f32[2,64,128]{2,1,0:T(8,128)} %copy-done.9) | copy-start | bytes 196612
  83.3 3.4 %copy-start.14 = (f32[2,64,127]{2,1,0:T(8,128)S(1)}, f32[2,64,127]{2,1,0:T(8,128)}, u32[]{:S(2)}) copy-start(f32[2,64,127]{2,1,0:T(8,128)} %slice.815) | copy-start | bytes 195076
  83.3 4.0 %copy-start.13 = (f32[2,64,128]{2,1,0:T(8,128)S(1)}, f32[2,64,128]{2,1,0:T(8,128)}, u32[]{:S(2)}) copy-start(f32[2,64,128]{2,1,0:T(8,128)} %copy-done.12) | copy-start | bytes 196612
  92.9 3.5 %copy-start.2 = (f32[3,8192]{0,1:T(8,128)S(1)}, f32[3,8192]{0,1:T(8,128)}, u32[]{:S(2)}) copy-start(f32[3,8192]{0,1:T(8,128)} %scatter_custom_fusion) | copy-start | bytes 294916
  92.9 3.5 %copy-start.24 = (f32[19,3,1]{0,1,2:T(4,128)S(1)}, f32[19,3,1]{0,1,2:T(4,128)}, u32[]{:S(2)}) copy-start(f32[19,3,1]{0,1,2:T(4,128)} %constant.84) | copy-start | bytes 688
  101.0 7.7 %copy-start.11 = (f32[2,64,128]{2,1,0:T(8,128)S(1)}, f32[2,64,128]{2,1,0:T(8,128)}, u32[]{:S(2)}) copy-start(f32[2,64,128]{2,1,0:T(8,128)} %get-tuple-element.81) | copy-start | bytes 196612
  103.1 13.4 %collective-permute-start = (f32[19,1,64,128]{3,2,1,0:T(8,128)}, f32[19,1,64,128]{3,2,1,0:T(8,128)}, u32[]{:S(2)}, u32[]{:S(2)}) collective-permute-start(f32[19,1,64,128]{3,2,1,0:T(8,128)} %get-tuple-element.80), channel_id=1, source_target_pairs={{0,1},{1,2},{2,3},{3,4},{4,5},{5,6},{6,7},{7,8},{8,9},{9,10},{10,1... | collective-permute-start | bytes 1867784 | tf_op jit(solution)/shard_map/ppermute | solution.py:44
  110.9 5.6 %copy-start.6 = (f32[19,64,128]{2,0,1:T(8,128)S(1)}, f32[19,64,128]{2,0,1:T(8,128)}, u32[]{:S(2)}) copy-start(f32[19,64,128]{2,0,1:T(8,128)} %fusion.172) | copy-start | bytes 1867780
  110.9 5.6 %copy-start.15 = (f32[64,128]{1,0:T(8,128)S(1)}, f32[64,128]{1,0:T(8,128)}, u32[]{:S(2)}) copy-start(f32[64,128]{1,0:T(8,128)} %multiply_bitcast_fusion.3) | copy-start | bytes 98308
  110.9 5.6 %copy-start.26 = (f32[19]{0:T(128)S(1)}, f32[19]{0:T(128)}, u32[]{:S(2)}) copy-start(f32[19]{0:T(128)} %constant.24.clone) | copy-start | bytes 232
  119.2 0.8 copy-start.7
  119.4 0.8 copy-start.19
  120.2 2.0 %copy-start.23 = (f32[19,3,1,1]{0,1,3,2:T(4,128)S(1)}, f32[19,3,1,1]{0,1,3,2:T(4,128)}, u32[]{:S(2)}) copy-start(f32[19,3,1,1]{0,1,3,2:T(4,128)} %constant.82) | copy-start | bytes 688
  123.7 0.7 copy-start.21
  126.7 2.5 %copy-start.16 = (pred[2,64,128]{2,1,0:T(8,128)(4,1)S(1)}, pred[2,64,128]{2,1,0:T(8,128)(4,1)}, u32[]{:S(2)}) copy-start(pred[2,64,128]{2,1,0:T(8,128)(4,1)} %get-tuple-element.37) | copy-start | bytes 49156
  126.7 2.7 %copy-start.18 = (pred[2,64,128]{2,1,0:T(8,128)(4,1)S(1)}, pred[2,64,128]{2,1,0:T(8,128)(4,1)}, u32[]{:S(2)}) copy-start(pred[2,64,128]{2,1,0:T(8,128)(4,1)} %get-tuple-element.35) | copy-start | bytes 49156
  126.8 2.7 %copy-start.17 = (pred[2,64,128]{2,1,0:T(8,128)(4,1)S(1)}, pred[2,64,128]{2,1,0:T(8,128)(4,1)}, u32[]{:S(2)}) copy-start(pred[2,64,128]{2,1,0:T(8,128)(4,1)} %get-tuple-element.33) | copy-start | bytes 49156
  126.8 16.1 %collective-permute-start.2 = (f32[19,1,64,128]{3,2,0,1:T(8,128)S(1)}, f32[19,1,64,128]{3,2,0,1:T(8,128)S(1)}, u32[]{:S(2)}, u32[]{:S(2)}) collective-permute-start(f32[19,1,64,128]{3,2,0,1:T(8,128)S(1)} %get-tuple-element.67), channel_id=1, source_target_pairs={{0,1},{1,2},{2,3},{3,4},{4,5},{5,6},{6,7},{7,8},{8,9},{9,10},{10,1... | collective-permute-start | bytes 1867784 | tf_op jit(solution)/shard_map/ppermute | solution.py:44
  129.6 13.7 %collective-permute-start.3 = (f32[19,1,64,128]{3,2,0,1:T(8,128)S(1)}, f32[19,1,64,128]{3,2,0,1:T(8,128)S(1)}, u32[]{:S(2)}, u32[]{:S(2)}) collective-permute-start(f32[19,1,64,128]{3,2,0,1:T(8,128)S(1)} %get-tuple-element.66), channel_id=1, source_target_pairs={{1,0},{2,1},{3,2},{4,3},{5,4},{6,5},{7,6},{8,7},{9,8},{10,9},{11,1... | collective-permute-start | bytes 1867784 | tf_op jit(solution)/shard_map/ppermute | solution.py:45
  145.1 1.0 copy-start.27
where the time goes:
time: 147 us; the launch traced here: 146 us
  blocking collectives  55.3 us (38%)
  other arithmetic  25.1 us (17%)
  matrix products  21.8 us (15%)
  local copies, waits for them, and re-layouts  20 us (14%)
  waiting for transfers between devices  11.2 us (8%)
  starting transfers between devices  10.4 us (7%)
  between operations  2.29 us (2%)
    psum x1, blocking collectives, body(): coefficients = lax.psum(partial_terms, 'ax')  31.4 us
    all_gather x1, blocking collectives, body(): whole_inflow = lax.all_gather(local_inflow, 'ax', axis=2, tiled=True)  23.9 us
    dot_general x4, matrix products, equilibrium(): jnp.einsum('iq,q...->i...', lattice, velocity, precision=lax.Precision.HI...  13.1 us
    ppermute x2, waiting for transfers between devices, extended(): before = lax.ppermute(last, axis, up)  11.2 us
    scatter x2, local copies, waits for them, and re-layouts, inlet_plane(): jnp.zeros((3, height * plane_width), jnp.float32).at[:, inlet_cells]  8.61 us
    reduce_sum x4, other arithmetic, equilibrium(): speed_sq = jnp.sum(velocity * velocity, axis=0)  7.34 us
    ppermute x2, starting transfers between devices, extended(): before = lax.ppermute(last, axis, up)  6.2 us
    dot_general x2, matrix products, collide(): jnp.einsum('mi,i...->m...', moment_rows(), populations, precision=lax.Pre...  4.7 us
  transfers between devices with their start and end apart: 4, of which 1 were waited for; matrix products, arithmetic and copies ran while one was open for 26% of the time, Pallas kernels for 0%

commit v1 on v0

--- a/solution.py
+++ b/solution.py
@@ -32,6 +32,19 @@
 relax_base = 0.52
 smagorinsky_sq = 0.04
 inflow_scale = 0.05
+
+
+def ring_gather(x, axis, dim):
+    ways = lax.axis_size(axis)
+    up = [(d, (d + 1) % ways) for d in range(ways)]
+    down = [(d, (d - 1) % ways) for d in range(ways)]
+    earlier, later = ([x], [x])
+    for _ in range(ways // 2):
+        earlier.append(lax.ppermute(earlier[-1], axis, up))
+    for _ in range((ways - 1) // 2):
+        later.append(lax.ppermute(later[-1], axis, down))
+    line = jnp.concatenate([*earlier[::-1], *later[1:]], axis=dim)
+    return jnp.roll(line, (lax.axis_index(axis) - ways // 2) * x.shape[dim], axis=dim)
 
 
 def extended(array, sides, width):
@@ -135,7 +148,7 @@
     local_inflow = jnp.einsum(
         "kjc,sk->sjc", pod_basis, coefficients, precision=lax.Precision.HIGHEST
     )
-    whole_inflow = lax.all_gather(local_inflow, "ax", axis=2, tiled=True)
+    whole_inflow = ring_gather(local_inflow, "ax", 2)
     position = lax.axis_index("ax")
     axis_count = lax.axis_size("ax")
     height = populations.shape[2]

time: 147 us -> 156 us (1.061)
  starting transfers between devices: 10.4 us -> 41.4 us
  blocking collectives: 55.3 us -> 30.6 us
  waiting for transfers between devices: 11.2 us -> 20.8 us
  other arithmetic: 25.1 us -> 19.7 us
  matrix products: 21.8 us -> 19.3 us
    ppermute x0 -> x15, starting transfers between devices: none -> 26.7 us  [the longest x7 22.3 us: ring_gather(): later.append(lax.ppermute(later[-1], axis, down))]
    all_gather x1 -> x0, blocking collectives: 23.9 us -> none  [body(): whole_inflow = lax.all_gather(local_inflow, 'ax', axis=2, tiled=True)]
    ppermute x0 -> x15, waiting for transfers between devices: none -> 8.42 us  [the longest x8 4.38 us: ring_gather(): earlier.append(lax.ppermute(earlier[-1], axis, up))]
    ppermute x2, starting transfers between devices: 4.16 us -> 8.19 us  [extended(): after = lax.ppermute(leading, axis, down)]
    dot_general x4, matrix products: 13.1 us -> 10.4 us  [equilibrium(): jnp.einsum('iq,q...->i...', lattice, velocity, precision=lax.Precision.HI...]
    mul x0 -> x2, local copies, waits for them, and re-layouts: none -> 2.43 us  [body(): inflow_scale * whole_inflow[segment_index]]
    select_n x2, other arithmetic: 2.13 us -> 0.21 us  [body(): jnp.where(position == axis_count - 1, relaxed[:, -1], ghost_high)]
    slice x42, local copies, waits for them, and re-layouts: 2.95 us -> 1.14 us  [stream(): source = jnp.roll(source, (step_y, step_x), axis=(1, 2))]
  transfers between devices with their start and end apart: 4 -> 19, of which waited for: 1 -> 9; matrix products, arithmetic and copies ran while one was open for 26% -> 29% of each run, Pallas kernels for 0% -> 0%
where the time goes in v1:
time: 156 us; the launch traced here: 155 us
  starting transfers between devices  41.4 us (27%)
  blocking collectives  30.6 us (20%)
  local copies, waits for them, and re-layouts  21.1 us (14%)
  waiting for transfers between devices  20.8 us (13%)
  other arithmetic  19.7 us (13%)
  matrix products  19.3 us (12%)
  between operations  2.38 us (2%)
    psum x1, blocking collectives, body(): coefficients = lax.psum(partial_terms, 'ax')  30.6 us
    ppermute x7, starting transfers between devices, ring_gather(): later.append(lax.ppermute(later[-1], axis, down))  22.3 us
    ppermute x2, waiting for transfers between devices, extended(): before = lax.ppermute(last, axis, up)  11.7 us
    dot_general x4, matrix products, equilibrium(): jnp.einsum('iq,q...->i...', lattice, velocity, precision=lax.Precision.HI...  10.4 us
    scatter x2, local copies, waits for them, and re-layouts, inlet_plane(): jnp.zeros((3, height * plane_width), jnp.float32).at[:, inlet_cells]  8.63 us
    ppermute x2, starting transfers between devices, extended(): after = lax.ppermute(leading, axis, down)  8.19 us
    reduce_sum x4, other arithmetic, equilibrium(): speed_sq = jnp.sum(velocity * velocity, axis=0)  7.31 us
    ppermute x2, starting transfers between devices, extended(): before = lax.ppermute(last, axis, up)  6.53 us
  transfers between devices with their start and end apart: 19, of which 9 were waited for; matrix products, arithmetic and copies ran while one was open for 29% of the time, Pallas kernels for 0%

profile of v1, /device:TPU:1, one launch (start us, length us, event | category | flops | bytes accessed | tf_op | source)
XLA Modules:
  0.0 155.2 jit_solution(8058942273767640119)
XLA Ops:
  1.4 1.0 fusion.141
  2.6 30.6 %psum.7 = f32[2,512]{1,0:T(2,128)S(1)} all-reduce(f32[2,512]{1,0:T(2,128)S(1)} %convolution_bitcast_fusion), channel_id=1, replica_groups=mesh['case'=2,'ax'=16] {'ax'}, use_global_device_ids=true, to_apply=%region_1.2 | all-reduce | flops 1024 | bytes 8192 | tf_op jit(solution)/shard_map/psum | solution.py:147
  33.6 1.1 collective-permute-start
  34.7 3.4 %collective-permute-start.8 = (f32[2,3,32]{2,0,1:T(2,128)S(1)}, f32[2,3,32]{2,0,1:T(2,128)S(1)}, u32[]{:S(2)}, u32[]{:S(2)}) collective-permute-start(f32[2,3,32]{2,0,1:T(2,128)S(1)} %fusion.139), channel_id=1, source_target_pairs={{0,15},{1,0},{2,1},{3,2},{4,3},{5,4},{6,5},{7,6},{8,7},{9,8},{10,9... | collective-permute-start | bytes 2312 | tf_op jit(solution)/shard_map/ppermute | solution.py:45
  38.1 3.0 %fusion.4 = f32[10,2,64,128]{3,0,2,1:T(8,128)S(1)} fusion(f32[10,19,1,1]{1,0,3,2:T(8,128)} %constant.107, f32[19,2,64,128]{3,2,1,0:T(8,128)} %param.19), kind=kOutput, calls=%fused_computation.12 | convolution fusion | flops 37355520 | bytes 1901304 | tf_op jit(solution)/shard_map/mi,i...->m.../dot_general | solution.py:87
  41.4 1.5 fusion.149
  43.4 0.8 copy-done.4
  44.2 2.8 %copy_subtract_fusion = f32[19,2,64,128]{3,0,2,1:T(8,128)S(1)} fusion(f32[19,2,64,128]{3,2,1,0:T(8,128)S(1)} %copy-done.4, f32[19,2,64,128]{3,2,1,0:T(8,128)S(1)} %get-tuple-element.100, f32[19,2,64,128]{3,2,1,0:T(8,128)S(1)} %get-tuple-element.61, f32[19,2,64,128]{3,0,2,1:T(8,128)S(1)} %fusion.149, f32[19,2,64,128]{3,2,1,0:T(8,128)S(1)} %get-tuple-element.60, ...), kind=kLoop, calls=%fused_computation.11 | loop fusion | flops 1556480 | bytes 7536640 | tf_op jit(solution)/shard_map/sub | solution.py:92
  47.1 0.9 fusion.171
  48.5 1.0 subtract_select_fusion
  49.7 0.9 copy-done.6
  50.6 0.9 slice.826
  51.5 6.3 %collective-permute-start.16 = (f32[19,1,64,128]{3,2,1,0:T(8,128)}, f32[19,1,64,128]{3,2,1,0:T(8,128)S(1)}, u32[]{:S(2)}, u32[]{:S(2)}) collective-permute-start(f32[19,1,64,128]{3,2,1,0:T(8,128)} %slice.826), channel_id=1, source_target_pairs={{1,0},{2,1},{3,2},{4,3},{5,4},{6,5},{7,6},{8,7},{9,8},{10,9},{11,1... | collective-permute-start | bytes 1867784 | tf_op jit(solution)/shard_map/ppermute | solution.py:58
  57.9 0.6 constant_dynamic-update-slice_fusion.17
  59.2 2.0 %collective-permute-start.2 = (f32[2,3,32]{2,0,1:T(2,128)S(1)}, f32[2,3,32]{2,0,1:T(2,128)S(1)}, u32[]{:S(2)}, u32[]{:S(2)}) collective-permute-start(f32[2,3,32]{2,0,1:T(2,128)S(1)} %collective-permute-done.1), channel_id=1, source_target_pairs={{0,1},{1,2},{2,3},{3,4},{4,5},{5,6},{6,7},{7,8},{8,9},{9,10},{10,1... | collective-permute-start | bytes 2312 | tf_op jit(solution)/shard_map/ppermute | solution.py:43
  61.3 0.6 constant_dynamic-update-slice_fusion.16
  61.9 1.4 collective-permute-done.9
  63.9 1.2 collective-permute-start.3
  65.0 0.6 constant_dynamic-update-slice_fusion.15
  65.7 0.6 collective-permute-done.10
  66.3 3.3 %collective-permute-start.11 = (f32[2,3,32]{2,0,1:T(2,128)S(1)}, f32[2,3,32]{2,0,1:T(2,128)}, u32[]{:S(2)}, u32[]{:S(2)}) collective-permute-start(f32[2,3,32]{2,0,1:T(2,128)S(1)} %collective-permute-done.10), channel_id=1, source_target_pairs={{0,15},{1,0},{2,1},{3,2},{4,3},{5,4},{6,5},{7,6},{8,7},{9,8},{10,9... | collective-permute-start | bytes 2312 | tf_op jit(solution)/shard_map/ppermute | solution.py:45
  69.6 0.6 constant_dynamic-update-slice_fusion.14
  70.5 4.8 %collective-permute-start.12 = (f32[2,3,32]{2,0,1:T(2,128)}, f32[2,3,32]{2,0,1:T(2,128)}, u32[]{:S(2)}, u32[]{:S(2)}) collective-permute-start(f32[2,3,32]{2,0,1:T(2,128)} %collective-permute-done.11), channel_id=1, source_target_pairs={{0,15},{1,0},{2,1},{3,2},{4,3},{5,4},{6,5},{7,6},{8,7},{9,8},{10,9... | collective-permute-start | bytes 2312 | tf_op jit(solution)/shard_map/ppermute | solution.py:45
  76.5 4.9 %collective-permute-start.13 = (f32[2,3,32]{2,0,1:T(2,128)}, f32[2,3,32]{2,0,1:T(2,128)}, u32[]{:S(2)}, u32[]{:S(2)}) collective-permute-start(f32[2,3,32]{2,0,1:T(2,128)} %collective-permute-done.12), channel_id=1, source_target_pairs={{0,15},{1,0},{2,1},{3,2},{4,3},{5,4},{6,5},{7,6},{8,7},{9,8},{10,9... | collective-permute-start | bytes 2312 | tf_op jit(solution)/shard_map/ppermute | solution.py:45
  81.4 1.1 collective-permute-done.13
  82.5 4.9 %collective-permute-start.14 = (f32[2,3,32]{2,0,1:T(2,128)}, f32[2,3,32]{2,0,1:T(2,128)}, u32[]{:S(2)}, u32[]{:S(2)}) collective-permute-start(f32[2,3,32]{2,0,1:T(2,128)} %collective-permute-done.13), channel_id=1, source_target_pairs={{0,15},{1,0},{2,1},{3,2},{4,3},{5,4},{6,5},{7,6},{8,7},{9,8},{10,9... | collective-permute-start | bytes 2312 | tf_op jit(solution)/shard_map/ppermute | solution.py:45
  87.4 1.7 %slice.866 = f32[1,2,64,128]{3,0,2,1:T(1,128)} slice(f32[19,2,64,128]{3,0,2,1:T(8,128)} %copy-done.6), slice={[18:19], [0:2], [0:64], [0:128]} | slice | bytes 131072 | tf_op jit(solution)/shard_map/slice | solution.py:122
  89.2 4.3 %collective-permute-done.7 = f32[2,3,32]{2,0,1:T(2,128)} collective-permute-done((f32[2,3,32]{2,0,1:T(2,128)}, f32[2,3,32]{2,0,1:T(2,128)}, u32[]{:S(2)}, u32[]{:S(2)}) %collective-permute-start.7) | collective-permute-done | bytes 800 | tf_op jit(solution)/shard_map/ppermute | solution.py:43
  93.5 1.0 concatenate.172
  94.5 0.7 dynamic-slice_multiply_fusion
  95.2 0.9 copy.98
  96.0 4.3 %scatter_custom_fusion = f32[3,8192]{0,1:T(8,128)} fusion(s32[512]{0:T(512)} %compare_select_fusion, f32[512,3]{1,0:T(8,128)} %copy.98, f32[]{:T(128)} %constant.36.clone.1), kind=kCustom, calls=%fused_computation.7 | custom fusion | bytes 98816 | tf_op jit(solution)/shard_map/scatter | solution.py:128
  100.4 3.3 %multiply_reduce_fusion.1 = f32[8192]{0:T(1024)S(1)} fusion(f32[3,8192]{0,1:T(8,128)} %scatter_custom_fusion), kind=kLoop, calls=%fused_computation.3 | loop fusion | flops 40960 | bytes 131072 | tf_op jit(solution)/shard_map/reduce_sum | solution.py:78
  104.3 1.6 %copy.132 = f32[512,3]{1,0:T(8,128)} copy(f32[512,3]{0,1:T(4,128)} %bitcast.650) | data formatting | bytes 12288 | tf_op jit(solution)/shard_map/mul | solution.py:159
  105.9 4.3 %scatter_custom_fusion.1 = f32[3,8192]{0,1:T(8,128)} fusion(s32[512]{0:T(512)} %compare_select_fusion, f32[512,3]{1,0:T(8,128)} %copy.132, f32[]{:T(128)} %constant.36.clone.1), kind=kCustom, calls=%fused_computation.5 | custom fusion | bytes 98816 | tf_op jit(solution)/shard_map/scatter | solution.py:128
  110.2 3.5 %multiply_reduce_fusion = f32[8192]{0:T(1024)S(1)} fusion(f32[3,8192]{0,1:T(8,128)} %scatter_custom_fusion.1), kind=kLoop, calls=%fused_computation.2 | loop fusion | flops 40960 | bytes 131072 | tf_op jit(solution)/shard_map/reduce_sum | solution.py:78
  113.7 3.7 %fusion.172 = f32[19,64,128]{2,0,1:T(8,128)S(1)} fusion(f32[19,3,1]{0,1,2:T(4,128)S(1)} %copy-done.25, f32[3,64,128]{0,2,1:T(8,128)S(1)} %bitcast.600), kind=kOutput, calls=%fused_computation.345 | convolution fusion | flops 5603328 | bytes 721124 | tf_op jit(solution)/shard_map/iq,q...->i.../dot_general | solution.py:77
  117.6 2.1 %collective-permute-start.15 = (f32[19,1,64,128]{3,2,1,0:T(8,128)S(1)}, f32[19,1,64,128]{3,2,1,0:T(8,128)S(1)}, u32[]{:S(2)}, u32[]{:S(2)}) collective-permute-start(f32[19,1,64,128]{3,2,1,0:T(8,128)S(1)} %get-tuple-element.80), channel_id=1, source_target_pairs={{0,1},{1,2},{2,3},{3,4},{4,5},{5,6},{6,7},{7,8},{8,9},{9,10},{10,1... | collective-permute-start | bytes 1867784 | tf_op jit(solution)/shard_map/ppermute | solution.py:57
  119.8 3.8 %fusion.173 = f32[19,64,128]{2,0,1:T(8,128)S(1)} fusion(f32[19,3,1]{0,1,2:T(4,128)S(1)} %copy-done.25, f32[3,64,128]{0,2,1:T(8,128)S(1)} %bitcast.599), kind=kOutput, calls=%fused_computation.346 | convolution fusion | flops 5603328 | bytes 721124 | tf_op jit(solution)/shard_map/iq,q...->i.../dot_general | solution.py:77
  123.6 3.1 %collective-permute-done.15 = f32[19,1,64,128]{3,2,1,0:T(8,128)S(1)} collective-permute-done((f32[19,1,64,128]{3,2,1,0:T(8,128)S(1)}, f32[19,1,64,128]{3,2,1,0:T(8,128)S(1)}, u32[]{:S(2)}, u32[]{:S(2)}) %collective-permute-start.15) | collective-permute-done | bytes 622624 | tf_op jit(solution)/shard_map/ppermute | solution.py:57
  129.3 1.7 %fusion.8 = f32[10,2,64,128]{3,0,2,1:T(8,128)S(1)} fusion(f32[10,19,1,1]{1,0,3,2:T(8,128)S(1)} %copy-done.12, f32[19,2,64,128]{3,2,1,0:T(8,128)S(1)} %get-tuple-element.2), kind=kOutput, calls=%fused_computation.16 | convolution fusion | flops 37355520 | bytes 1901304 | tf_op jit(solution)/shard_map/mi,i...->m.../dot_general | solution.py:87
  131.1 1.5 fusion.150
  133.5 1.6 %fusion.6 = f32[6,2,64,128]{3,0,2,1:T(8,128)S(1)} fusion(f32[6,19,1,1]{1,0,3,2:T(8,128)S(1)} %copy-done.16, f32[19,2,64,128]{3,2,1,0:T(8,128)S(1)} %fusion.14), kind=kOutput, calls=%fused_computation.14 | convolution fusion | flops 22413312 | bytes 1638856 | tf_op jit(solution)/shard_map/mi,i...->m.../dot_general | solution.py:93
  136.0 4.4 %collective-permute-start.17 = (f32[19,1,64,128]{3,2,0,1:T(8,128)S(1)}, f32[19,1,64,128]{3,2,0,1:T(8,128)S(1)}, u32[]{:S(2)}, u32[]{:S(2)}) collective-permute-start(f32[19,1,64,128]{3,2,0,1:T(8,128)S(1)} %get-tuple-element.67), channel_id=1, source_target_pairs={{0,1},{1,2},{2,3},{3,4},{4,5},{5,6},{6,7},{7,8},{8,9},{9,10},{10,1... | collective-permute-start | bytes 1867784 | tf_op jit(solution)/shard_map/ppermute | solution.py:57
  140.8 1.9 %collective-permute-start.18 = (f32[19,1,64,128]{3,2,0,1:T(8,128)S(1)}, f32[19,1,64,128]{3,2,0,1:T(8,128)S(1)}, u32[]{:S(2)}, u32[]{:S(2)}) collective-permute-start(f32[19,1,64,128]{3,2,0,1:T(8,128)S(1)} %get-tuple-element.66), channel_id=1, source_target_pairs={{1,0},{2,1},{3,2},{4,3},{5,4},{6,5},{7,6},{8,7},{9,8},{10,9},{11,1... | collective-permute-start | bytes 1867784 | tf_op jit(solution)/shard_map/ppermute | solution.py:58
  142.8 8.5 %collective-permute-done.17 = f32[19,1,64,128]{3,2,0,1:T(8,128)S(1)} collective-permute-done((f32[19,1,64,128]{3,2,0,1:T(8,128)S(1)}, f32[19,1,64,128]{3,2,0,1:T(8,128)S(1)}, u32[]{:S(2)}, u32[]{:S(2)}) %collective-permute-start.17) | collective-permute-done | bytes 622624 | tf_op jit(solution)/shard_map/ppermute | solution.py:57
  151.6 0.7 collective-permute-done.18
  154.2 1.0 copy-done.28
  (189 shorter events, 12.3 us)
Async XLA Ops:
  0.6 1.7 %copy-start = (f32[512,3,32]{0,2,1:T(8,128)S(1)}, f32[512,3,32]{0,2,1:T(8,128)}, u32[]{:S(2)}) copy-start(f32[512,3,32]{0,2,1:T(8,128)} %param.23) | copy-start | bytes 589828
  33.6 59.9 %copy-start.13 = (f32[2,3,32]{2,0,1:T(2,128)}, f32[2,3,32]{2,0,1:T(2,128)S(1)}, u32[]{:S(2)}) copy-start(f32[2,3,32]{2,0,1:T(2,128)S(1)} %fusion.139) | copy-start | bytes 2308
  33.6 7.8 %copy-start.23 = (f32[19,3,1,1]{0,1,3,2:T(4,128)S(1)}, f32[19,3,1,1]{0,1,3,2:T(4,128)}, u32[]{:S(2)}) copy-start(f32[19,3,1,1]{0,1,3,2:T(4,128)} %constant.108) | copy-start | bytes 688
  33.6 24.3 %collective-permute-start = (f32[2,3,32]{2,0,1:T(2,128)S(1)}, f32[2,3,32]{2,0,1:T(2,128)S(1)}, u32[]{:S(2)}, u32[]{:S(2)}) collective-permute-start(f32[2,3,32]{2,0,1:T(2,128)S(1)} %fusion.139), channel_id=1, source_target_pairs={{0,1},{1,2},{2,3},{3,4},{4,5},{5,6},{6,7},{7,8},{8,9},{9,10},{10,1... | collective-permute-start | bytes 2312 | tf_op jit(solution)/shard_map/ppermute | solution.py:43
  34.7 24.0 %collective-permute-start.8 = (f32[2,3,32]{2,0,1:T(2,128)S(1)}, f32[2,3,32]{2,0,1:T(2,128)S(1)}, u32[]{:S(2)}, u32[]{:S(2)}) collective-permute-start(f32[2,3,32]{2,0,1:T(2,128)S(1)} %fusion.139), channel_id=1, source_target_pairs={{0,15},{1,0},{2,1},{3,2},{4,3},{5,4},{6,5},{7,6},{8,7},{9,8},{10,9... | collective-permute-start | bytes 2312 | tf_op jit(solution)/shard_map/ppermute | solution.py:45
  41.4 1.5 copy-start.26
  42.9 1.3 copy-start.4
  44.2 2.8 %copy-start.15 = (f32[6,19,1,1]{1,0,3,2:T(8,128)S(1)}, f32[6,19,1,1]{1,0,3,2:T(8,128)}, u32[]{:S(2)}) copy-start(f32[6,19,1,1]{1,0,3,2:T(8,128)} %constant.109) | copy-start | bytes 1372
  47.1 1.3 copy-start.1
  49.4 1.2 copy-start.6
  50.6 7.3 %copy-start.5 = (s32[2,2,64,128]{3,2,1,0:T(8,128)S(1)}, s32[2,2,64,128]{3,2,1,0:T(8,128)}, u32[]{:S(2)}) copy-start(s32[2,2,64,128]{3,2,1,0:T(8,128)} %param.21) | copy-start | bytes 393220
  51.5 66.0 %collective-permute-start.16 = (f32[19,1,64,128]{3,2,1,0:T(8,128)}, f32[19,1,64,128]{3,2,1,0:T(8,128)S(1)}, u32[]{:S(2)}, u32[]{:S(2)}) collective-permute-start(f32[19,1,64,128]{3,2,1,0:T(8,128)} %slice.826), channel_id=1, source_target_pairs={{1,0},{2,1},{3,2},{4,3},{5,4},{6,5},{7,6},{8,7},{9,8},{10,9},{11,1... | collective-permute-start | bytes 1867784 | tf_op jit(solution)/shard_map/ppermute | solution.py:58
  57.8 17.6 %copy-start.29 = (s32[512]{0:T(512)S(1)}, s32[512]{0:T(512)}, u32[]{:S(2)}) copy-start(s32[512]{0:T(512)} %param.22) | copy-start | bytes 6148
  57.9 1.4 collective-permute-start.1
  58.7 30.5 %copy-start.17 = (f32[2,3,32]{2,0,1:T(2,128)}, f32[2,3,32]{2,0,1:T(2,128)S(1)}, u32[]{:S(2)}) copy-start(f32[2,3,32]{2,0,1:T(2,128)S(1)} %collective-permute-done.8) | copy-start | bytes 2308
  58.7 4.6 %collective-permute-start.9 = (f32[2,3,32]{2,0,1:T(2,128)S(1)}, f32[2,3,32]{2,0,1:T(2,128)S(1)}, u32[]{:S(2)}, u32[]{:S(2)}) collective-permute-start(f32[2,3,32]{2,0,1:T(2,128)S(1)} %collective-permute-done.8), channel_id=1, source_target_pairs={{0,15},{1,0},{2,1},{3,2},{4,3},{5,4},{6,5},{7,6},{8,7},{9,8},{10,9... | collective-permute-start | bytes 2312 | tf_op jit(solution)/shard_map/ppermute | solution.py:45
  59.2 29.9 %copy-start.18 = (f32[2,3,32]{2,0,1:T(2,128)}, f32[2,3,32]{2,0,1:T(2,128)S(1)}, u32[]{:S(2)}) copy-start(f32[2,3,32]{2,0,1:T(2,128)S(1)} %collective-permute-done.1) | copy-start | bytes 2308
  59.2 4.6 %collective-permute-start.2 = (f32[2,3,32]{2,0,1:T(2,128)S(1)}, f32[2,3,32]{2,0,1:T(2,128)S(1)}, u32[]{:S(2)}, u32[]{:S(2)}) collective-permute-start(f32[2,3,32]{2,0,1:T(2,128)S(1)} %collective-permute-done.1), channel_id=1, source_target_pairs={{0,1},{1,2},{2,3},{3,4},{4,5},{5,6},{6,7},{7,8},{8,9},{9,10},{10,1... | collective-permute-start | bytes 2312 | tf_op jit(solution)/shard_map/ppermute | solution.py:43
  63.3 25.9 %copy-start.19 = (f32[2,3,32]{2,0,1:T(2,128)}, f32[2,3,32]{2,0,1:T(2,128)S(1)}, u32[]{:S(2)}) copy-start(f32[2,3,32]{2,0,1:T(2,128)S(1)} %collective-permute-done.9) | copy-start | bytes 2308
  63.3 3.0 %collective-permute-start.10 = (f32[2,3,32]{2,0,1:T(2,128)S(1)}, f32[2,3,32]{2,0,1:T(2,128)S(1)}, u32[]{:S(2)}, u32[]{:S(2)}) collective-permute-start(f32[2,3,32]{2,0,1:T(2,128)S(1)} %collective-permute-done.9), channel_id=1, source_target_pairs={{0,15},{1,0},{2,1},{3,2},{4,3},{5,4},{6,5},{7,6},{8,7},{9,8},{10,9... | collective-permute-start | bytes 2312 | tf_op jit(solution)/shard_map/ppermute | solution.py:45
  63.9 25.3 %copy-start.20 = (f32[2,3,32]{2,0,1:T(2,128)}, f32[2,3,32]{2,0,1:T(2,128)S(1)}, u32[]{:S(2)}) copy-start(f32[2,3,32]{2,0,1:T(2,128)S(1)} %collective-permute-done.2) | copy-start | bytes 2308
  63.9 5.7 %collective-permute-start.3 = (f32[2,3,32]{2,0,1:T(2,128)S(1)}, f32[2,3,32]{2,0,1:T(2,128)S(1)}, u32[]{:S(2)}, u32[]{:S(2)}) collective-permute-start(f32[2,3,32]{2,0,1:T(2,128)S(1)} %collective-permute-done.2), channel_id=1, source_target_pairs={{0,1},{1,2},{2,3},{3,4},{4,5},{5,6},{6,7},{7,8},{8,9},{9,10},{10,1... | collective-permute-start | bytes 2312 | tf_op jit(solution)/shard_map/ppermute | solution.py:43
  66.3 22.9 %copy-start.21 = (f32[2,3,32]{2,0,1:T(2,128)}, f32[2,3,32]{2,0,1:T(2,128)S(1)}, u32[]{:S(2)}) copy-start(f32[2,3,32]{2,0,1:T(2,128)S(1)} %collective-permute-done.10) | copy-start | bytes 2308
  66.3 4.2 %collective-permute-start.11 = (f32[2,3,32]{2,0,1:T(2,128)S(1)}, f32[2,3,32]{2,0,1:T(2,128)}, u32[]{:S(2)}, u32[]{:S(2)}) collective-permute-start(f32[2,3,32]{2,0,1:T(2,128)S(1)} %collective-permute-done.10), channel_id=1, source_target_pairs={{0,15},{1,0},{2,1},{3,2},{4,3},{5,4},{6,5},{7,6},{8,7},{9,8},{10,9... | collective-permute-start | bytes 2312 | tf_op jit(solution)/shard_map/ppermute | solution.py:45
  69.6 19.6 %copy-start.22 = (f32[2,3,32]{2,0,1:T(2,128)}, f32[2,3,32]{2,0,1:T(2,128)S(1)}, u32[]{:S(2)}) copy-start(f32[2,3,32]{2,0,1:T(2,128)S(1)} %collective-permute-done.3) | copy-start | bytes 2308
  69.6 5.8 %collective-permute-start.4 = (f32[2,3,32]{2,0,1:T(2,128)S(1)}, f32[2,3,32]{2,0,1:T(2,128)}, u32[]{:S(2)}, u32[]{:S(2)}) collective-permute-start(f32[2,3,32]{2,0,1:T(2,128)S(1)} %collective-permute-done.3), channel_id=1, source_target_pairs={{0,1},{1,2},{2,3},{3,4},{4,5},{5,6},{6,7},{7,8},{8,9},{9,10},{10,1... | collective-permute-start | bytes 2312 | tf_op jit(solution)/shard_map/ppermute | solution.py:43
  70.5 5.9 %collective-permute-start.12 = (f32[2,3,32]{2,0,1:T(2,128)}, f32[2,3,32]{2,0,1:T(2,128)}, u32[]{:S(2)}, u32[]{:S(2)}) collective-permute-start(f32[2,3,32]{2,0,1:T(2,128)} %collective-permute-done.11), channel_id=1, source_target_pairs={{0,15},{1,0},{2,1},{3,2},{4,3},{5,4},{6,5},{7,6},{8,7},{9,8},{10,9... | collective-permute-start | bytes 2312 | tf_op jit(solution)/shard_map/ppermute | solution.py:45
  75.4 6.0 %collective-permute-start.5 = (f32[2,3,32]{2,0,1:T(2,128)}, f32[2,3,32]{2,0,1:T(2,128)}, u32[]{:S(2)}, u32[]{:S(2)}) collective-permute-start(f32[2,3,32]{2,0,1:T(2,128)} %collective-permute-done.4), channel_id=1, source_target_pairs={{0,1},{1,2},{2,3},{3,4},{4,5},{5,6},{6,7},{7,8},{8,9},{9,10},{10,1... | collective-permute-start | bytes 2312 | tf_op jit(solution)/shard_map/ppermute | solution.py:43
  76.5 6.0 %collective-permute-start.13 = (f32[2,3,32]{2,0,1:T(2,128)}, f32[2,3,32]{2,0,1:T(2,128)}, u32[]{:S(2)}, u32[]{:S(2)}) collective-permute-start(f32[2,3,32]{2,0,1:T(2,128)} %collective-permute-done.12), channel_id=1, source_target_pairs={{0,15},{1,0},{2,1},{3,2},{4,3},{5,4},{6,5},{7,6},{8,7},{9,8},{10,9... | collective-permute-start | bytes 2312 | tf_op jit(solution)/shard_map/ppermute | solution.py:45
  81.4 6.0 %collective-permute-start.6 = (f32[2,3,32]{2,0,1:T(2,128)}, f32[2,3,32]{2,0,1:T(2,128)}, u32[]{:S(2)}, u32[]{:S(2)}) collective-permute-start(f32[2,3,32]{2,0,1:T(2,128)} %collective-permute-done.5), channel_id=1, source_target_pairs={{0,1},{1,2},{2,3},{3,4},{4,5},{5,6},{6,7},{7,8},{8,9},{9,10},{10,1... | collective-permute-start | bytes 2312 | tf_op jit(solution)/shard_map/ppermute | solution.py:43
  82.5 6.6 %collective-permute-start.14 = (f32[2,3,32]{2,0,1:T(2,128)}, f32[2,3,32]{2,0,1:T(2,128)}, u32[]{:S(2)}, u32[]{:S(2)}) collective-permute-start(f32[2,3,32]{2,0,1:T(2,128)} %collective-permute-done.13), channel_id=1, source_target_pairs={{0,15},{1,0},{2,1},{3,2},{4,3},{5,4},{6,5},{7,6},{8,7},{9,8},{10,9... | collective-permute-start | bytes 2312 | tf_op jit(solution)/shard_map/ppermute | solution.py:45
  87.4 6.0 %collective-permute-start.7 = (f32[2,3,32]{2,0,1:T(2,128)}, f32[2,3,32]{2,0,1:T(2,128)}, u32[]{:S(2)}, u32[]{:S(2)}) collective-permute-start(f32[2,3,32]{2,0,1:T(2,128)} %collective-permute-done.6), channel_id=1, source_target_pairs={{0,1},{1,2},{2,3},{3,4},{4,5},{5,6},{6,7},{7,8},{8,9},{9,10},{10,1... | collective-permute-start | bytes 2312 | tf_op jit(solution)/shard_map/ppermute | solution.py:43
  100.4 3.4 %copy-start.14 = (f32[1,3,512]{2,0,1:T(1,128)S(1)}, f32[1,3,512]{2,0,1:T(1,128)}, u32[]{:S(2)}) copy-start(f32[1,3,512]{2,0,1:T(1,128)} %get-tuple-element.98) | copy-start | bytes 18436
  110.2 3.5 %copy-start.3 = (f32[3,8192]{0,1:T(8,128)S(1)}, f32[3,8192]{0,1:T(8,128)}, u32[]{:S(2)}) copy-start(f32[3,8192]{0,1:T(8,128)} %scatter_custom_fusion) | copy-start | bytes 294916
  110.2 3.5 %copy-start.25 = (f32[19,3,1]{0,1,2:T(4,128)S(1)}, f32[19,3,1]{0,1,2:T(4,128)}, u32[]{:S(2)}) copy-start(f32[19,3,1]{0,1,2:T(4,128)} %constant.110) | copy-start | bytes 688
  113.7 6.1 %copy-start.2 = (f32[3,8192]{0,1:T(8,128)S(1)}, f32[3,8192]{0,1:T(8,128)}, u32[]{:S(2)}) copy-start(f32[3,8192]{0,1:T(8,128)} %scatter_custom_fusion.1) | copy-start | bytes 294916
  117.6 9.1 %collective-permute-start.15 = (f32[19,1,64,128]{3,2,1,0:T(8,128)S(1)}, f32[19,1,64,128]{3,2,1,0:T(8,128)S(1)}, u32[]{:S(2)}, u32[]{:S(2)}) collective-permute-start(f32[19,1,64,128]{3,2,1,0:T(8,128)S(1)} %get-tuple-element.80), channel_id=1, source_target_pairs={{0,1},{1,2},{2,3},{3,4},{4,5},{5,6},{6,7},{7,8},{8,9},{9,10},{10,1... | collective-permute-start | bytes 1867784 | tf_op jit(solution)/shard_map/ppermute | solution.py:57
  119.8 6.9 %copy-start.27 = (f32[19]{0:T(128)S(1)}, f32[19]{0:T(128)}, u32[]{:S(2)}) copy-start(f32[19]{0:T(128)} %constant.101.clone) | copy-start | bytes 232
  128.4 0.8 copy-start.7
  128.5 0.8 copy-start.12
  129.3 1.8 %copy-start.24 = (f32[19,3,1,1]{0,1,3,2:T(4,128)S(1)}, f32[19,3,1,1]{0,1,3,2:T(4,128)}, u32[]{:S(2)}) copy-start(f32[19,3,1,1]{0,1,3,2:T(4,128)} %constant.108) | copy-start | bytes 688
  135.8 4.6 %copy-start.9 = (pred[2,64,128]{2,1,0:T(8,128)(4,1)S(1)}, pred[2,64,128]{2,1,0:T(8,128)(4,1)}, u32[]{:S(2)}) copy-start(pred[2,64,128]{2,1,0:T(8,128)(4,1)} %get-tuple-element.37) | copy-start | bytes 49156
  135.8 4.8 %copy-start.10 = (pred[2,64,128]{2,1,0:T(8,128)(4,1)S(1)}, pred[2,64,128]{2,1,0:T(8,128)(4,1)}, u32[]{:S(2)}) copy-start(pred[2,64,128]{2,1,0:T(8,128)(4,1)} %get-tuple-element.35) | copy-start | bytes 49156
  135.9 4.8 %copy-start.11 = (pred[2,64,128]{2,1,0:T(8,128)(4,1)S(1)}, pred[2,64,128]{2,1,0:T(8,128)(4,1)}, u32[]{:S(2)}) copy-start(pred[2,64,128]{2,1,0:T(8,128)(4,1)} %get-tuple-element.33) | copy-start | bytes 49156
  135.9 6.8 %copy-start.8 = (pred[2,64,128]{2,1,0:T(8,128)(4,1)S(1)}, pred[2,64,128]{2,1,0:T(8,128)(4,1)}, u32[]{:S(2)}) copy-start(pred[2,64,128]{2,1,0:T(8,128)(4,1)} %get-tuple-element.31) | copy-start | bytes 49156
  136.0 15.3 %collective-permute-start.17 = (f32[19,1,64,128]{3,2,0,1:T(8,128)S(1)}, f32[19,1,64,128]{3,2,0,1:T(8,128)S(1)}, u32[]{:S(2)}, u32[]{:S(2)}) collective-permute-start(f32[19,1,64,128]{3,2,0,1:T(8,128)S(1)} %get-tuple-element.67), channel_id=1, source_target_pairs={{0,1},{1,2},{2,3},{3,4},{4,5},{5,6},{6,7},{7,8},{8,9},{9,10},{10,1... | collective-permute-start | bytes 1867784 | tf_op jit(solution)/shard_map/ppermute | solution.py:57
  140.8 11.6 %collective-permute-start.18 = (f32[19,1,64,128]{3,2,0,1:T(8,128)S(1)}, f32[19,1,64,128]{3,2,0,1:T(8,128)S(1)}, u32[]{:S(2)}, u32[]{:S(2)}) collective-permute-start(f32[19,1,64,128]{3,2,0,1:T(8,128)S(1)} %get-tuple-element.66), channel_id=1, source_target_pairs={{1,0},{2,1},{3,2},{4,3},{5,4},{6,5},{7,6},{8,7},{9,8},{10,9},{11,1... | collective-permute-start | bytes 1867784 | tf_op jit(solution)/shard_map/ppermute | solution.py:58
  154.2 1.0 copy-start.28
  (1 other events, 0.7 us)
